TPU v7x, 32 devices: a whole 2x2x4 slice. The times are simulated.
32 devices in a mesh: pat: 8 (over y, x, core), src: 4 (over z).
Axes of the slice: x: 2, y: 2, z: 4, core: 2. Of those that a mesh axis runs over, the one named last changes fastest.
Arguments:
- patterns: bfloat16 [8192, 12288], P('src', 'pat'), may hold values from -6 to 6
- left_factors: bfloat16 [3, 8, 512, 1024], P(None, 'src', 'pat'), may hold values from -0.125 to 0.125
- right_factors: bfloat16 [3, 8, 512, 1024], P(None, 'src', 'pat'), may hold values from -0.1875 to 0.1875
- ranks: int32 [3, 8], replicated, may hold values from 128 to 512, as said below
- source_slot_tile: int32 [8], replicated, may hold values from 0 to 7, each once
Outputs:
- potentials: float32 [3072, 12288], P('src', 'pat')
Inputs may be any that keep to these rules, and one draw needn't show every extreme that they name: `ranks`: some tile has rank exactly 512 and some exactly 128. `source_slot_tile`: every source tile is held by exactly one slot.
All inputs are finite; a program needn't handle non-finite values.
Results may differ from a plain program's by a relative error of at most 0.01.
Values may be sent and summed in bfloat16 or wider, within the bound.
No kernel may reach another device: no remote copies, remote signals or barrier semaphores. Data moves between devices by JAX's collectives and lax.ppermute only.
A program may use at most 576 MiB of HBM per device.

v0:
```python
import jax
import jax.numpy as jnp
from jax import lax
from jax.sharding import PartitionSpec as P


def body(patterns, left_factors, right_factors, ranks, source_slot_tile):
    trows, slots, rank_cols, tile = left_factors.shape
    rank_width = patterns.shape[1]
    slab_pieces = patterns.reshape(slots, tile, rank_width)
    total_slots = source_slot_tile.shape[0]
    slot_here = lax.axis_index("src") * slots + jnp.arange(slots, dtype=jnp.int32)
    catalog = jnp.arange(total_slots, dtype=jnp.int32)
    pick_slot = (catalog[None, :] == slot_here[:, None]).astype(jnp.int32)
    tile_here = jnp.sum(pick_slot * source_slot_tile[None, :], axis=1)
    pick_tile = (catalog[None, :] == tile_here[:, None]).astype(jnp.int32)
    rank_here = jnp.sum(ranks[:, None, :] * pick_tile[None, :, :], axis=2)
    piece = lax.all_gather(right_factors, "pat", axis=2, tiled=True)
    count = piece.shape[2]
    rows = jnp.arange(count, dtype=jnp.int32)
    coef = jnp.einsum("tsrb,sbp->tsrp", piece, slab_pieces, preferred_element_type=jnp.float32)
    live = rows[None, None, :] < rank_here[:, :, None]
    coef = jnp.where(live[..., None], coef, 0.0).astype(jnp.bfloat16)
    piece = lax.all_gather(left_factors, "pat", axis=2, tiled=True)
    total = jnp.einsum("tsrb,tsrp->tbp", piece, coef, preferred_element_type=jnp.float32)
    partial_value = total.reshape(trows * tile, rank_width)
    return lax.psum_scatter(
        partial_value.astype(jnp.bfloat16), "src", scatter_dimension=0, tiled=True
    ).astype(jnp.float32)


def solution(mesh):
    in_specs = (P("src", "pat"), P(None, "src", "pat", None), P(None, "src", "pat", None), P(), P())
    out_specs = P("src", "pat")
    return jax.shard_map(body, mesh=mesh, in_specs=in_specs, out_specs=out_specs, check_vma=False)
```

profile of v0, /device:TPU:0, one launch (start us, length us, event | category | flops | bytes accessed | tf_op | source)
XLA Modules:
  0.0 303.1 jit_solution(10433320378242377923)
XLA Ops:
  6.5 0.0 all-gather.5.cloned.1.call-start
  6.5 0.7 all-gather.5.cloned.1.call-update
  7.3 0.0 all-gather.3.cloned.1.call-start
  7.3 0.7 all-gather.3.cloned.1.call-update
  8.0 0.0 reduce-scatter.2.cloned.1.call-start
  8.1 0.8 fusion.9
  8.9 0.1 compare_convert_fusion
  9.0 0.8 multiply_reduce_fusion
  9.8 0.1 iota_compare_fusion
  9.9 47.5 %all-gather.5.cloned.1.call-done = bf16[3,2,512,1024]{3,2,1,0:T(8,128)(2,1)} async-done(((bf16[3,2,64,1024]{3,2,1,0:T(8,128)(2,1)}), bf16[3,2,512,1024]{3,2,1,0:T(8,128)(2,1)}) %all-gather.5.cloned.1.call-update) | async-done | bytes 6291472 | tf_op jit(solution)/shard_map/all_gather | solution.py:24
  57.4 47.3 %all-gather.3.cloned.1.call-done = bf16[3,2,512,1024]{3,2,1,0:T(8,128)(2,1)} async-done(((bf16[3,2,64,1024]{3,2,1,0:T(8,128)(2,1)}), bf16[3,2,512,1024]{3,2,1,0:T(8,128)(2,1)}) %all-gather.3.cloned.1.call-update) | async-done | bytes 6291472 | tf_op jit(solution)/shard_map/all_gather | solution.py:18
  104.7 26.0 %bitcast_convert_fusion = bf16[3,1536,1024]{1,2,0:T(8,128)(2,1)} fusion(bf16[3,2,512,1024]{3,2,1,0:T(8,128)(2,1)} %all-gather.5.cloned.1.call-done, pred[3,2,512]{2,1,0:T(4,128)(4,1)S(1)} %iota_compare_fusion, bf16[2,1024,1536,1]{2,1,0,3:T(8,128)(2,1)} %bitcast.20, bf16[3,2,512,1024]{3,2,1,0:T(8,128)(2,1)} %all-gather.3.cloned.1.call-done), kind=kOutput, calls=%fused_computation | convolution fusion | flops 19341508608 | bytes 28314624 | tf_op jit(solution)/shard_map/tsrb,tsrp->tbp/dot_general | solution.py:25
  130.7 0.0 reduce-scatter.2.cloned.1.call-update
  130.8 161.3 %reduce-scatter.2.cloned.1.call-done = bf16[768,1536]{1,0:T(8,128)(2,1)} async-done(((bf16[3072,1536]{1,0:T(8,128)(2,1)}), bf16[768,1536]{1,0:T(8,128)(2,1)}) %reduce-scatter.2.cloned.1.call-update) | async-done | bytes 2359312 | tf_op jit(solution)/shard_map/reduce_scatter | solution.py:27
  292.1 4.5 %convert_element_type.28 = f32[768,1536]{1,0:T(8,128)} convert(bf16[768,1536]{1,0:T(8,128)(2,1)} %reduce-scatter.2.cloned.1.call-done) | non-fusion elementwise | flops 1179648 | bytes 7077888 | tf_op jit(solution)/shard_map/convert_element_type | solution.py:29
  (1 shorter events, 0.0 us)
Async XLA Ops:
  6.5 50.8 %all-gather.5.cloned.1.call-start = ((), (), s32[]{:S(2)}) async-start(), calls=%async_computation.2 | async-start | bytes 7077888 | tf_op jit(solution)/shard_map/all_gather | solution.py:24
  7.3 97.5 %all-gather.3.cloned.1.call-start = ((), (), s32[]{:S(2)}) async-start(), calls=%async_computation.1 | async-start | bytes 7077888 | tf_op jit(solution)/shard_map/all_gather | solution.py:18
  8.0 284.1 %reduce-scatter.2.cloned.1.call-start = ((), (), s32[]{:S(2)}) async-start(), calls=%async_computation.3 | async-start | bytes 11796480 | tf_op jit(solution)/shard_map/reduce_scatter | solution.py:27
Sparse Core Ops, SparseCore 0:
  9.2 48.1 all-gather.4
  59.3 45.3 all-gather.2
  130.9 161.1 reduce-scatter.1
where the time goes:
time: 303 us
  waiting for transfers between devices  258 us (85%)
  matrix products  26 us (9%)
  between operations  13.1 us (4%)
  other arithmetic  6.32 us (2%)
    reduce_scatter x1, waiting for transfers between devices, body(): lax.psum_scatter(partial_value.astype(jnp.bfloat16), 'src', scatter_dimen...  161 us
    all_gather x1, waiting for transfers between devices, body(): piece = lax.all_gather(left_factors, 'pat', axis=2, tiled=True)  47.5 us
    all_gather x1, waiting for transfers between devices, body(): piece = lax.all_gather(right_factors, 'pat', axis=2, tiled=True)  47.3 us
    dot_general x1, matrix products, body(): jnp.einsum('tsrb,tsrp->tbp', piece, coef, preferred_element_type=jnp.floa...  26 us
  transfers between devices with their start and end apart: 3, of which 3 were waited for; matrix products, arithmetic and copies ran while one was open for 1% of the time, Pallas kernels for 0%

commit v1 on v0

--- a/solution.py
+++ b/solution.py
@@ -2,6 +2,17 @@
 import jax.numpy as jnp
 from jax import lax
 from jax.sharding import PartitionSpec as P
+
+
+def collect(value, axis, dim):
+    ways = lax.axis_size(axis)
+    pieces = [value]
+    for far in range(1, ways):
+        pieces.append(
+            lax.ppermute(pieces[far - 1], axis, [(d, (d - 1) % ways) for d in range(ways)])
+        )
+    line = jnp.concatenate(pieces, axis=dim)
+    return jnp.roll(line, lax.axis_index(axis) * value.shape[dim], axis=dim)
 
 
 def body(patterns, left_factors, right_factors, ranks, source_slot_tile):
@@ -21,7 +32,7 @@
     coef = jnp.einsum("tsrb,sbp->tsrp", piece, slab_pieces, preferred_element_type=jnp.float32)
     live = rows[None, None, :] < rank_here[:, :, None]
     coef = jnp.where(live[..., None], coef, 0.0).astype(jnp.bfloat16)
-    piece = lax.all_gather(left_factors, "pat", axis=2, tiled=True)
+    piece = collect(left_factors, "pat", 2)
     total = jnp.einsum("tsrb,tsrp->tbp", piece, coef, preferred_element_type=jnp.float32)
     partial_value = total.reshape(trows * tile, rank_width)
     return lax.psum_scatter(

time: 303 us -> 354 us (1.17)
  local copies, waits for them, and re-layouts: 0 us -> 50.1 us
  waiting for transfers between devices: 258 us -> 233 us
  starting transfers between devices: 0.08 us -> 20.5 us
    ppermute x0 -> x7, waiting for transfers between devices: none -> 71.3 us  [collect(): lax.ppermute(pieces[far - 1], axis, [(d, (d - 1) % ways) for d in range(w...]
    all_gather x1 -> x0, waiting for transfers between devices: 47.5 us -> none  [body(): piece = lax.all_gather(left_factors, 'pat', axis=2, tiled=True)]
    all_gather x1, waiting for transfers between devices: 47.3 us -> 0.02 us  [body(): piece = lax.all_gather(right_factors, 'pat', axis=2, tiled=True)]
    concatenate x0 -> x1, local copies, waits for them, and re-layouts: none -> 28.1 us  [collect(): return jnp.roll(line, lax.axis_index(axis) * value.shape[dim], axis=dim)]
    ppermute x0 -> x7, starting transfers between devices: none -> 20.4 us  [collect(): lax.ppermute(pieces[far - 1], axis, [(d, (d - 1) % ways) for d in range(w...]
    ppermute x0 -> x7, local copies, waits for them, and re-layouts: none -> 16.6 us  [collect(): lax.ppermute(pieces[far - 1], axis, [(d, (d - 1) % ways) for d in range(w...]
    unnamed x0 -> x11, local copies, waits for them, and re-layouts: none -> 5.37 us
  transfers between devices with their start and end apart: 3 -> 9, of which waited for: 3 -> 7; matrix products, arithmetic and copies ran while one was open for 1% -> 14% of each run, Pallas kernels for 0% -> 0%
where the time goes in v1:
time: 354 us; the launch traced here: 351 us
  waiting for transfers between devices  233 us (66%)
  local copies, waits for them, and re-layouts  50.1 us (14%)
  matrix products  27.4 us (8%)
  starting transfers between devices  20.5 us (6%)
  between operations  13.5 us (4%)
  other arithmetic  6.31 us (2%)
    reduce_scatter x1, waiting for transfers between devices, body(): lax.psum_scatter(partial_value.astype(jnp.bfloat16), 'src', scatter_dimen...  161 us
    ppermute x7, waiting for transfers between devices, collect(): lax.ppermute(pieces[far - 1], axis, [(d, (d - 1) % ways) for d in range(w...  71.3 us
    concatenate x1, local copies, waits for them, and re-layouts, collect(): return jnp.roll(line, lax.axis_index(axis) * value.shape[dim], axis=dim)  28.1 us
    dot_general x1, matrix products, body(): jnp.einsum('tsrb,tsrp->tbp', piece, coef, preferred_element_type=jnp.floa...  27.4 us
    ppermute x7, starting transfers between devices, collect(): lax.ppermute(pieces[far - 1], axis, [(d, (d - 1) % ways) for d in range(w...  20.4 us
    ppermute x7, local copies, waits for them, and re-layouts, collect(): lax.ppermute(pieces[far - 1], axis, [(d, (d - 1) % ways) for d in range(w...  16.6 us
  transfers between devices with their start and end apart: 9, of which 7 were waited for; matrix products, arithmetic and copies ran while one was open for 14% of the time, Pallas kernels for 0%

profile of v1, /device:TPU:0, one launch (start us, length us, event | category | flops | bytes accessed | tf_op | source)
XLA Modules:
  0.0 351.1 jit_solution(11420012886367738226)
XLA Ops:
  6.5 0.0 all-gather.2.cloned.1.call-start
  6.5 0.7 all-gather.2.cloned.1.call-update
  7.3 0.0 reduce-scatter.2.cloned.1.call-start
  7.3 3.4 collective-permute-start
  10.7 10.4 %collective-permute-done = bf16[3,2,64,1024]{3,2,1,0:T(8,128)(2,1)S(1)} collective-permute-done((bf16[3,2,64,1024]{3,2,1,0:T(8,128)(2,1)}, bf16[3,2,64,1024]{3,2,1,0:T(8,128)(2,1)S(1)}, u32[]{:S(2)}, u32[]{:S(2)}) %collective-permute-start) | collective-permute-done | bytes 786464 | tf_op jit(solution)/shard_map/ppermute | solution.py:12
  21.1 0.0 copy-start
  21.1 0.9 copy-done
  22.0 2.7 collective-permute-start.1
  24.7 12.6 %collective-permute-done.1 = bf16[3,2,64,1024]{3,2,1,0:T(8,128)(2,1)S(1)} collective-permute-done((bf16[3,2,64,1024]{3,2,1,0:T(8,128)(2,1)S(1)}, bf16[3,2,64,1024]{3,2,1,0:T(8,128)(2,1)S(1)}, u32[]{:S(2)}, u32[]{:S(2)}) %collective-permute-start.1) | collective-permute-done | bytes 786464 | tf_op jit(solution)/shard_map/ppermute | solution.py:12
  37.3 0.0 copy-start.1
  37.3 0.9 copy-done.1
  38.2 2.9 collective-permute-start.2
  41.1 20.4 %collective-permute-done.2 = bf16[3,2,64,1024]{3,2,1,0:T(8,128)(2,1)S(1)} collective-permute-done((bf16[3,2,64,1024]{3,2,1,0:T(8,128)(2,1)S(1)}, bf16[3,2,64,1024]{3,2,1,0:T(8,128)(2,1)S(1)}, u32[]{:S(2)}, u32[]{:S(2)}) %collective-permute-start.2) | collective-permute-done | bytes 786464 | tf_op jit(solution)/shard_map/ppermute | solution.py:12
  61.5 0.0 copy-start.2
  61.5 0.9 copy-done.2
  62.4 2.9 collective-permute-start.3
  65.3 10.7 %collective-permute-done.3 = bf16[3,2,64,1024]{3,2,1,0:T(8,128)(2,1)S(1)} collective-permute-done((bf16[3,2,64,1024]{3,2,1,0:T(8,128)(2,1)S(1)}, bf16[3,2,64,1024]{3,2,1,0:T(8,128)(2,1)S(1)}, u32[]{:S(2)}, u32[]{:S(2)}) %collective-permute-start.3) | collective-permute-done | bytes 786464 | tf_op jit(solution)/shard_map/ppermute | solution.py:12
  75.9 0.0 copy-start.3
  75.9 0.9 copy-done.3
  76.8 2.9 collective-permute-start.4
  79.7 9.5 %collective-permute-done.4 = bf16[3,2,64,1024]{3,2,1,0:T(8,128)(2,1)S(1)} collective-permute-done((bf16[3,2,64,1024]{3,2,1,0:T(8,128)(2,1)S(1)}, bf16[3,2,64,1024]{3,2,1,0:T(8,128)(2,1)S(1)}, u32[]{:S(2)}, u32[]{:S(2)}) %collective-permute-start.4) | collective-permute-done | bytes 786464 | tf_op jit(solution)/shard_map/ppermute | solution.py:12
  89.2 0.0 copy-start.4
  89.2 2.8 collective-permute-start.5
  92.0 1.8 copy.25
  93.8 7.7 %collective-permute-done.5 = bf16[3,2,64,1024]{3,2,1,0:T(8,128)(2,1)} collective-permute-done((bf16[3,2,64,1024]{3,2,1,0:T(8,128)(2,1)S(1)}, bf16[3,2,64,1024]{3,2,1,0:T(8,128)(2,1)}, u32[]{:S(2)}, u32[]{:S(2)}) %collective-permute-start.5) | collective-permute-done | bytes 786464 | tf_op jit(solution)/shard_map/ppermute | solution.py:12
  101.5 2.9 collective-permute-start.6
  104.4 0.8 fusion.10
  105.3 0.1 compare_convert_fusion
  105.3 0.8 multiply_reduce_fusion
  106.2 0.0 copy-done.4
  106.2 0.1 iota_compare_fusion
  106.3 1.8 copy.26
  108.1 2.5 copy.27
  110.5 2.5 copy.28
  113.0 2.5 copy.29
  115.5 2.5 copy.30
  118.0 2.5 copy.31
  120.4 0.0 collective-permute-done.6
  120.4 2.5 copy.32
  122.9 28.1 %concatenate.6 = bf16[3,2,1024,1024]{2,3,1,0:T(8,128)(2,1)} concatenate(bf16[3,2,64,1024]{2,3,1,0:T(8,128)(2,1)S(1)} %copy.25, bf16[3,2,64,1024]{2,3,1,0:T(8,128)(2,1)S(1)} %copy.26, bf16[3,2,64,1024]{2,3,1,0:T(8,128)(2,1)} %copy.27, bf16[3,2,64,1024]{2,3,1,0:T(8,128)(2,1)} %copy.28, bf16[3,2,64,1024]{2,3,1,0:T(8,128)(2,1)} %copy.29, bf16[3,2,64,1024]{2,3,1,0:T(8,128)(2,1)} %copy.30, ...), dimensions={2} | concatenate | bytes 25165824 | tf_op jit(solution)/shard_map/jit(_roll_dynamic)/concatenate | solution.py:15
  151.0 0.0 all-gather.2.cloned.1.call-done
  151.0 27.4 %bitcast_convert_fusion = bf16[3,1024,1536]{2,1,0:T(8,128)(2,1)} fusion(pred[3,2,512]{2,1,0:T(4,128)(4,1)S(1)} %iota_compare_fusion, bf16[3,2,1024,1024]{2,3,1,0:T(8,128)(2,1)} %concatenate.6, s32[]{:T(128)S(6)} %select_n.18, bf16[2,1024,1536,1]{2,1,0,3:T(8,128)(2,1)} %bitcast.17, bf16[3,2,512,1024]{3,2,1,0:T(8,128)(2,1)} %all-gather.2.cloned.1.call-done), kind=kOutput, calls=%fused_computation | convolution fusion | flops 19341508608 | bytes 28314628 | tf_op jit(solution)/shard_map/tsrb,tsrp->tbp/dot_general | solution.py:36
  178.4 0.0 reduce-scatter.2.cloned.1.call-update
  178.4 161.3 %reduce-scatter.2.cloned.1.call-done = bf16[768,1536]{1,0:T(8,128)(2,1)} async-done(((bf16[3072,1536]{1,0:T(8,128)(2,1)}), bf16[768,1536]{1,0:T(8,128)(2,1)}) %reduce-scatter.2.cloned.1.call-update) | async-done | bytes 2359312 | tf_op jit(solution)/shard_map/reduce_scatter | solution.py:38
  339.7 4.5 %convert_element_type.24 = f32[768,1536]{1,0:T(8,128)} convert(bf16[768,1536]{1,0:T(8,128)(2,1)} %reduce-scatter.2.cloned.1.call-done) | non-fusion elementwise | flops 1179648 | bytes 7077888 | tf_op jit(solution)/shard_map/convert_element_type | solution.py:40
  (1 shorter events, 0.0 us)
Async XLA Ops:
  6.5 144.4 %all-gather.2.cloned.1.call-start = ((), (), s32[]{:S(2)}) async-start(), calls=%async_computation.1 | async-start | bytes 7077888 | tf_op jit(solution)/shard_map/all_gather | solution.py:29
  7.3 332.5 %reduce-scatter.2.cloned.1.call-start = ((), (), s32[]{:S(2)}) async-start(), calls=%async_computation.2 | async-start | bytes 11796480 | tf_op jit(solution)/shard_map/reduce_scatter | solution.py:38
  7.3 13.8 %collective-permute-start = (bf16[3,2,64,1024]{3,2,1,0:T(8,128)(2,1)}, bf16[3,2,64,1024]{3,2,1,0:T(8,128)(2,1)S(1)}, u32[]{:S(2)}, u32[]{:S(2)}) collective-permute-start(bf16[3,2,64,1024]{3,2,1,0:T(8,128)(2,1)} %param.6), channel_id=1, source_target_pairs={{0,28},{4,0},{8,4},{12,8},{16,12},{20,16},{24,20},{28,24},{1,29},{... | collective-permute-start | bytes 2359304 | tf_op jit(solution)/shard_map/ppermute | solution.py:12
  21.1 0.9 copy-start
  22.0 15.3 %collective-permute-start.1 = (bf16[3,2,64,1024]{3,2,1,0:T(8,128)(2,1)S(1)}, bf16[3,2,64,1024]{3,2,1,0:T(8,128)(2,1)S(1)}, u32[]{:S(2)}, u32[]{:S(2)}) collective-permute-start(bf16[3,2,64,1024]{3,2,1,0:T(8,128)(2,1)S(1)} %collective-permute-done), channel_id=1, source_target_pairs={{0,28},{4,0},{8,4},{12,8},{16,12},{20,16},{24,20},{28,24},{1,29},{... | collective-permute-start | bytes 2359304 | tf_op jit(solution)/shard_map/ppermute | solution.py:12
  37.3 0.9 copy-start.1
  38.2 23.3 %collective-permute-start.2 = (bf16[3,2,64,1024]{3,2,1,0:T(8,128)(2,1)S(1)}, bf16[3,2,64,1024]{3,2,1,0:T(8,128)(2,1)S(1)}, u32[]{:S(2)}, u32[]{:S(2)}) collective-permute-start(bf16[3,2,64,1024]{3,2,1,0:T(8,128)(2,1)S(1)} %collective-permute-done.1), channel_id=1, source_target_pairs={{0,28},{4,0},{8,4},{12,8},{16,12},{20,16},{24,20},{28,24},{1,29},{... | collective-permute-start | bytes 2359304 | tf_op jit(solution)/shard_map/ppermute | solution.py:12
  61.5 0.9 copy-start.2
  62.4 13.5 %collective-permute-start.3 = (bf16[3,2,64,1024]{3,2,1,0:T(8,128)(2,1)S(1)}, bf16[3,2,64,1024]{3,2,1,0:T(8,128)(2,1)S(1)}, u32[]{:S(2)}, u32[]{:S(2)}) collective-permute-start(bf16[3,2,64,1024]{3,2,1,0:T(8,128)(2,1)S(1)} %collective-permute-done.2), channel_id=1, source_target_pairs={{0,28},{4,0},{8,4},{12,8},{16,12},{20,16},{24,20},{28,24},{1,29},{... | collective-permute-start | bytes 2359304 | tf_op jit(solution)/shard_map/ppermute | solution.py:12
  75.9 0.9 copy-start.3
  76.8 12.4 %collective-permute-start.4 = (bf16[3,2,64,1024]{3,2,1,0:T(8,128)(2,1)S(1)}, bf16[3,2,64,1024]{3,2,1,0:T(8,128)(2,1)S(1)}, u32[]{:S(2)}, u32[]{:S(2)}) collective-permute-start(bf16[3,2,64,1024]{3,2,1,0:T(8,128)(2,1)S(1)} %collective-permute-done.3), channel_id=1, source_target_pairs={{0,28},{4,0},{8,4},{12,8},{16,12},{20,16},{24,20},{28,24},{1,29},{... | collective-permute-start | bytes 2359304 | tf_op jit(solution)/shard_map/ppermute | solution.py:12
  89.2 17.0 %copy-start.4 = (bf16[3,2,64,1024]{3,2,1,0:T(8,128)(2,1)}, bf16[3,2,64,1024]{3,2,1,0:T(8,128)(2,1)S(1)}, u32[]{:S(2)}) copy-start(bf16[3,2,64,1024]{3,2,1,0:T(8,128)(2,1)S(1)} %collective-permute-done.4) | copy-start | bytes 2359300
  89.2 12.3 %collective-permute-start.5 = (bf16[3,2,64,1024]{3,2,1,0:T(8,128)(2,1)S(1)}, bf16[3,2,64,1024]{3,2,1,0:T(8,128)(2,1)}, u32[]{:S(2)}, u32[]{:S(2)}) collective-permute-start(bf16[3,2,64,1024]{3,2,1,0:T(8,128)(2,1)S(1)} %collective-permute-done.4), channel_id=1, source_target_pairs={{0,28},{4,0},{8,4},{12,8},{16,12},{20,16},{24,20},{28,24},{1,29},{... | collective-permute-start | bytes 2359304 | tf_op jit(solution)/shard_map/ppermute | solution.py:12
  101.5 18.9 %collective-permute-start.6 = (bf16[3,2,64,1024]{3,2,1,0:T(8,128)(2,1)}, bf16[3,2,64,1024]{3,2,1,0:T(8,128)(2,1)}, u32[]{:S(2)}, u32[]{:S(2)}) collective-permute-start(bf16[3,2,64,1024]{3,2,1,0:T(8,128)(2,1)} %collective-permute-done.5), channel_id=1, source_target_pairs={{0,28},{4,0},{8,4},{12,8},{16,12},{20,16},{24,20},{28,24},{1,29},{... | collective-permute-start | bytes 2359304 | tf_op jit(solution)/shard_map/ppermute | solution.py:12
Sparse Core Ops, SparseCore 0:
  9.2 62.7 all-gather.1
  178.5 161.1 reduce-scatter.1
